TPU v7x, 256 devices: a whole 4x4x8 slice. The times are simulated.
256 devices in a mesh: seq: 32 (over z_hi, y, core), tp: 8 (over z_lo, x).
Axes of the slice: x: 4, y: 4, z: 8 (z_hi: 4, z_lo: 2; z = z_hi * 2 + z_lo), core: 2. Of those that a mesh axis runs over, the one named last changes fastest.
Arguments:
- hidden_sel: bfloat16 [8192, 7168], P('seq', 'tp'), may hold values from -6 to 6
- w_query: bfloat16 [7168, 4096], P(None, 'tp'), may hold values from -0.0625 to 0.0625
- w_key: bfloat16 [7168, 1024], P(None, 'tp'), may hold values from -0.0625 to 0.0625
- w_value: bfloat16 [7168, 1024], P(None, 'tp'), may hold values from -0.0625 to 0.0625
- key_cache: bfloat16 [65536, 1024], P('seq', 'tp')
- value_cache: bfloat16 [65536, 1024], P('seq', 'tp'), may hold values from -6 to 6
- span_count: int32 [8], replicated, may hold values from 1 to 8, 32 in all
- span_key: int32 [8, 8], replicated, may hold values from 0 to 7, each once within a row
- cache_offset: int32 [64], P('seq'), may hold values from 0 to 8191
- sel_index: int32 [64, 128], P('seq'), may hold values from 0 to 1023, as said below
Outputs:
- attn_out: bfloat16 [8192, 4096], P('seq', 'tp')
Inputs may be any that keep to these rules, and one draw needn't show every extreme that they name: `sel_index`: each row holds 128 different positions in rising order. `span_count`: the counts sum to 32, and the largest is exactly 8. `span_key`: each row is a permutation of 0 to 7.
All inputs are finite; a program needn't handle non-finite values.
Results may differ from a plain program's by a relative error of at most 0.023.
Values may be sent and summed in bfloat16 or wider, within the bound.
No kernel may reach another device: no remote copies, remote signals or barrier semaphores. Data moves between devices by JAX's collectives and lax.ppermute only.
A program may use at most 128 MiB of HBM per device.

v0:
```python
import math

import jax
import jax.numpy as jnp
from jax import lax
from jax.sharding import PartitionSpec as P

HD = 128
HG = 4
R = 8
MAXCH = 8
SPAN = 1024
SEL = 128


rope_base = 5000000.0
masked_score = -1e30


def passed_along(value, axis, steps):
    count = lax.axis_size(axis)
    pairs = [(source, (source + steps) % count) for source in range(count)]
    return lax.ppermute(value, axis, pairs)


def rotate(values, angle):
    half = values.shape[-1] // 2
    first = values[..., :half]
    second = values[..., half:]
    cosine = jnp.cos(angle)
    sine = jnp.sin(angle)
    return jnp.concatenate(
        [first * cosine - second * sine, second * cosine + first * sine], axis=-1
    )


def frequencies(width):
    return rope_base ** (-(jnp.arange(width // 2, dtype=jnp.float32) * 2.0) / width)


def span_ranks(span_count, span_key):
    column = jnp.arange(MAXCH, dtype=jnp.int32)
    filled = column[None, :] < span_count[:, None]
    earlier = span_key[:, :, None] < span_key[:, None, :]
    ranks = jnp.sum((earlier & filled[:, :, None]).astype(jnp.int32), axis=1, dtype=jnp.int32)
    return (filled.T.reshape(-1), ranks.T.reshape(-1))


def shards(
    hidden_sel,
    w_query,
    w_key,
    w_value,
    key_cache,
    value_cache,
    span_count,
    span_key,
    cache_offset,
    sel_index,
):
    slots = sel_index.shape[0]
    heads = w_key.shape[1] // HD
    seq_size = lax.axis_size("seq")
    stride = R // slots
    index = lax.axis_index("seq")
    piece = lax.all_gather(hidden_sel, "tp", axis=1, tiled=True)
    query_full = jnp.dot(piece, w_query, preferred_element_type=jnp.float32)
    key_full = jnp.dot(piece, w_key, preferred_element_type=jnp.float32)
    value_full = jnp.dot(piece, w_value, preferred_element_type=jnp.float32)
    filled_all, rank_all = span_ranks(span_count, span_key)
    first_slot = index * slots
    filled_q = lax.dynamic_slice_in_dim(filled_all, first_slot, slots)
    rank_q = lax.dynamic_slice_in_dim(rank_all, first_slot, slots)
    freq = frequencies(HD)
    new_pos = rank_q[:, None] * SPAN + sel_index
    angle = new_pos.astype(jnp.float32)[:, :, None] * freq
    query = rotate(
        query_full.reshape(slots, SEL, heads, HG, HD), angle[:, :, None, None, :]
    ).astype(jnp.bfloat16)
    query = jnp.transpose(query, (0, 2, 1, 3, 4)).reshape(slots, heads, SEL * HG, HD)
    new_key = rotate(key_full.reshape(slots, SEL, heads, HD), angle[:, :, None, :]).astype(
        jnp.bfloat16
    )
    new_value = value_full.astype(jnp.bfloat16).reshape(slots, SEL, heads, HD)
    delta = rank_q * SPAN - cache_offset
    angle_delta = delta.astype(jnp.float32)[:, None, None, None] * freq
    cached = rotate(
        key_cache.reshape(slots, SPAN, heads, HD).astype(jnp.float32), angle_delta
    ).astype(jnp.bfloat16)
    slot_ids = jnp.broadcast_to(jnp.arange(slots, dtype=jnp.int32)[:, None], (slots, SEL))
    joined_key = cached.at[slot_ids, sel_index].set(new_key)
    joined_value = (
        value_cache.reshape(slots, SPAN, heads, HD).at[slot_ids, sel_index].set(new_value)
    )
    local_block = jnp.stack(
        [jnp.transpose(joined_key, (0, 2, 1, 3)), jnp.transpose(joined_value, (0, 2, 1, 3))]
    )
    column = jnp.arange(SPAN, dtype=jnp.int32)
    scale = 1.0 / math.sqrt(HD)

    def lookup(source):
        filled_k = lax.dynamic_slice_in_dim(filled_all, source * slots, slots)
        rank_k = lax.dynamic_slice_in_dim(rank_all, source * slots, slots)
        return (filled_k, rank_k)

    def update(state, qblock, qpos, block, source):
        top, total, acc = state
        filled_k, rank_k = lookup(source)
        key_pos = rank_k[:, None] * SPAN + column[None, :]
        allowed = filled_k[:, None, None, None] & (
            key_pos[:, None, None, :] <= qpos[:, None, :, None]
        )
        scores = jnp.einsum("bhqd,bhkd->bhqk", qblock, block[0], preferred_element_type=jnp.float32)
        scores = jnp.where(allowed, scores * scale, masked_score)
        new_top = jnp.maximum(top, jnp.max(scores, axis=-1))
        factor = jnp.exp(top - new_top)
        weight = jnp.exp(scores - new_top[..., None])
        total = total * factor + jnp.sum(weight, axis=-1)
        acc = acc * factor[..., None] + jnp.einsum(
            "bhqk,bhkd->bhqd",
            weight.astype(jnp.bfloat16),
            block[1],
            preferred_element_type=jnp.float32,
        )
        return (new_top, total, acc)

    def attend(state, qblock, qsource, qsel, block, source):
        filled_x, rank_x = lookup(qsource)
        qpos = jnp.repeat(rank_x[:, None] * SPAN + qsel, HG, axis=1)
        return update(state, qblock, qpos, block, source)

    initial = (
        jnp.full((slots, heads, SEL * HG), masked_score, jnp.float32),
        jnp.zeros((slots, heads, SEL * HG), jnp.float32),
        jnp.zeros((slots, heads, SEL * HG, HD), jnp.float32),
    )
    state = attend(initial, query, index, sel_index, local_block, index)
    moving = local_block
    for step in range(1, MAXCH):
        moving = passed_along(moving, "seq", stride)
        state = attend(state, query, index, sel_index, moving, (index - step * stride) % seq_size)
    top, total, acc = state
    mixed = acc / total[..., None]
    mixed = jnp.where(filled_q[:, None, None, None], mixed, 0.0).astype(jnp.bfloat16)
    mixed = mixed.reshape(slots, heads, SEL, HG, HD)
    return jnp.transpose(mixed, (0, 2, 1, 3, 4)).reshape(slots * SEL, heads * HG * HD)


def solution(mesh):
    placed = (
        P("seq", "tp"),
        P(None, "tp"),
        P(None, "tp"),
        P(None, "tp"),
        P("seq", "tp"),
        P("seq", "tp"),
        P(),
        P(),
        P("seq"),
        P("seq", None),
    )
    return jax.shard_map(
        shards, mesh=mesh, in_specs=placed, out_specs=P("seq", "tp"), check_vma=False
    )
```

profile of v0, /device:TPU:132, one launch (start us, length us, event | category | flops | bytes accessed | tf_op | source)
XLA Modules:
  0.0 487.6 jit_solution(3857587526153206929)
XLA Ops:
  6.5 0.7 all-gather.2.cloned.1.call-update
  7.4 0.8 iota_compare_fusion.1
  8.2 0.9 convert_reduce_fusion
  9.2 1.1 convert.27
  10.4 0.8 dynamic-slice_multiply_fusion
  11.3 0.4 subtract_convert_fusion
  11.7 0.3 maximum_bitcast_fusion
  12.1 46.3 %all-gather.2.cloned.1.call-done = bf16[256,7168]{1,0:T(8,128)(2,1)} async-done(((bf16[256,896]{1,0:T(8,128)(2,1)}), bf16[256,7168]{1,0:T(8,128)(2,1)}) %all-gather.2.cloned.1.call-update) | async-done | bytes 3670032 | tf_op jit(solution)/shard_map/all_gather | solution.py:66
  58.4 3.4 fusion.144
  61.8 0.6 fusion.114
  62.5 1.1 convolution_convert_fusion
  63.6 12.5 %scatter_fusion.1 = bf16[2,1024,128]{2,1,0:T(8,128)(2,1)S(1)} fusion(bf16[2,1024,128]{2,1,0:T(8,128)(2,1)S(1)} %bitcast.84, s32[256]{0:T(256)S(1)} %fusion.119, bf16[256,128]{1,0:T(8,128)(2,1)S(1)} %convolution_convert_fusion), kind=kCustom, calls=%fused_computation.1 | custom fusion | bytes 198656 | tf_op jit(solution)/shard_map/scatter | solution.py:93
  76.1 12.5 %scatter_fusion = bf16[2,1024,128]{2,1,0:T(8,128)(2,1)S(1)} fusion(bf16[2,1024,128]{2,1,0:T(8,128)(2,1)S(1)} %maximum_bitcast_fusion, s32[256]{0:T(256)S(1)} %fusion.119, bf16[256,128]{1,0:T(8,128)(2,1)S(1)} %bitcast.89), kind=kCustom, calls=%fused_computation | custom fusion | bytes 198656 | tf_op jit(solution)/shard_map/scatter | solution.py:91
  88.7 3.0 collective-permute-start
  91.7 48.8 %collective-permute-done = bf16[2,2,1,1024,128]{4,3,1,2,0:T(8,128)(2,1)S(1)} collective-permute-done((bf16[2,2,1,1024,128]{4,3,1,2,0:T(8,128)(2,1)S(1)}, bf16[2,2,1,1024,128]{4,3,1,2,0:T(8,128)(2,1)S(1)}, u32[]{:S(2)}, u32[]{:S(2)}) %collective-permute-start) | collective-permute-done | bytes 1048608 | tf_op jit(solution)/shard_map/ppermute | solution.py:23
  140.5 1.0 copy-done.10
  141.5 71.0 %collective-permute-done.1 = bf16[2,2,1,1024,128]{4,3,1,2,0:T(8,128)(2,1)S(1)} collective-permute-done((bf16[2,2,1,1024,128]{4,3,1,2,0:T(8,128)(2,1)S(1)}, bf16[2,2,1,1024,128]{4,3,1,2,0:T(8,128)(2,1)S(1)}, u32[]{:S(2)}, u32[]{:S(2)}) %collective-permute-start.1) | collective-permute-done | bytes 1048608 | tf_op jit(solution)/shard_map/ppermute | solution.py:23
  212.6 52.1 %collective-permute-done.2 = bf16[2,2,1,1024,128]{4,3,1,2,0:T(8,128)(2,1)S(1)} collective-permute-done((bf16[2,2,1,1024,128]{4,3,1,2,0:T(8,128)(2,1)S(1)}, bf16[2,2,1,1024,128]{4,3,1,2,0:T(8,128)(2,1)S(1)}, u32[]{:S(2)}, u32[]{:S(2)}) %collective-permute-start.2) | collective-permute-done | bytes 1048608 | tf_op jit(solution)/shard_map/ppermute | solution.py:23
  265.0 0.1 le.45
  265.4 0.5 multiply_cosine_fusion.1
  266.0 70.5 %collective-permute-done.3 = bf16[2,2,1,1024,128]{4,3,1,2,0:T(8,128)(2,1)} collective-permute-done((bf16[2,2,1,1024,128]{4,3,1,2,0:T(8,128)(2,1)S(1)}, bf16[2,2,1,1024,128]{4,3,1,2,0:T(8,128)(2,1)}, u32[]{:S(2)}, u32[]{:S(2)}) %collective-permute-start.3) | collective-permute-done | bytes 1048608 | tf_op jit(solution)/shard_map/ppermute | solution.py:23
  336.5 6.2 %fusion.143 = f32[256,512]{1,0:T(8,128)S(1)} fusion(bf16[256,7168]{1,0:T(8,128)(2,1)} %all-gather.2.cloned.1.call-done, bf16[7168,512]{1,0:T(8,128)(2,1)} %param.11), kind=kOutput, calls=%fused_computation.181 | convolution fusion | flops 1879048192 | bytes 11534336 | tf_op jit(solution)/shard_map/dot_general | solution.py:67
  342.7 0.2 reshape.1044
  342.9 0.5 subtract_convert_fusion.1
  343.4 0.1 pad_maximum_fusion.1
  343.6 1.5 fusion.16
  345.1 42.1 %collective-permute-done.4 = bf16[2,2,1,1024,128]{4,3,1,2,0:T(8,128)(2,1)} collective-permute-done((bf16[2,2,1,1024,128]{4,3,1,2,0:T(8,128)(2,1)}, bf16[2,2,1,1024,128]{4,3,1,2,0:T(8,128)(2,1)}, u32[]{:S(2)}, u32[]{:S(2)}) %collective-permute-start.4) | collective-permute-done | bytes 1048608 | tf_op jit(solution)/shard_map/ppermute | solution.py:23
  387.1 0.7 fusion.107
  387.8 0.7 fusion.106
  388.6 1.7 fusion.105
  390.3 26.6 %collective-permute-done.5 = bf16[2,2,1,1024,128]{4,3,1,2,0:T(8,128)(2,1)S(1)} collective-permute-done((bf16[2,2,1,1024,128]{4,3,1,2,0:T(8,128)(2,1)}, bf16[2,2,1,1024,128]{4,3,1,2,0:T(8,128)(2,1)S(1)}, u32[]{:S(2)}, u32[]{:S(2)}) %collective-permute-start.5) | collective-permute-done | bytes 1048608 | tf_op jit(solution)/shard_map/ppermute | solution.py:23
  416.9 6.9 %fusion = (f32[2,512]{1,0:T(2,128)S(1)}, f32[2,512]{1,0:T(2,128)S(1)}, f32[2,512]{1,0:T(2,128)S(1)}, f32[2,512]{1,0:T(2,128)S(1)}, f32[2,512]{1,0:T(2,128)S(1)}, /*index=5*/f32[2,512,1024]{2,1,0:T(8,128)}) fusion(f32[2,512,1024]{2,1,0:T(8,128)S(1)} %get-tuple-element.69, f32[2,512]{1,0:T(2,128)S(1)} %broadcast_maximum_fusion, s32[2,512]{1,0:T(2,128)S(1)} %le.45, ...), kind=kOutput, calls=%fused_computation.18 | convolution fusion | flops 295693312 | bytes 21830144 | tf_op jit(solution)/shard_map/bhqd,bhkd->bhqk/dot_general | solution.py:113
  423.9 0.7 fusion.103
  424.6 21.1 %collective-permute-done.6 = bf16[2,2,1,1024,128]{4,3,1,2,0:T(8,128)(2,1)S(1)} collective-permute-done((bf16[2,2,1,1024,128]{4,3,1,2,0:T(8,128)(2,1)S(1)}, bf16[2,2,1,1024,128]{4,3,1,2,0:T(8,128)(2,1)S(1)}, u32[]{:S(2)}, u32[]{:S(2)}) %collective-permute-start.6) | collective-permute-done | bytes 1048608 | tf_op jit(solution)/shard_map/ppermute | solution.py:23
  445.7 0.7 fusion.102
  446.4 7.9 %fusion.2 = (f32[2,512]{1,0:T(2,128)S(1)}, f32[2,512]{1,0:T(2,128)S(1)}, f32[2,512]{1,0:T(2,128)S(1)}, f32[2,512]{1,0:T(2,128)S(1)}, f32[2,512]{1,0:T(2,128)S(1)}, /*index=5*/f32[2,512,1024]{2,1,0:T(8,128)S(1)}) fusion(f32[2,512,1024]{2,1,0:T(8,128)} %get-tuple-element.70, f32[2,512]{1,0:T(2,128)S(1)} %get-tuple-element.33, ...), kind=kOutput, calls=%fused_computation.20 | convolution fusion | flops 296741888 | bytes 21831690 | tf_op jit(solution)/shard_map/bhqd,bhkd->bhqk/dot_general | solution.py:113
  454.3 1.8 fusion.14
  456.1 6.4 %fusion.6 = (f32[2,512]{1,0:T(2,128)S(1)}, f32[2,512]{1,0:T(2,128)S(1)}, f32[2,512]{1,0:T(2,128)S(1)}, f32[2,512]{1,0:T(2,128)S(1)}) fusion(f32[2,512,1024]{2,1,0:T(8,128)S(1)} %fusion.106, f32[2,512]{1,0:T(2,128)S(1)} %get-tuple-element.31, s32[2,1024]{1,0:T(2,128)S(1)} %get-tuple-element.76, s32[2,512]{1,0:T(2,128)S(1)} %le.45, ...), kind=kLoop, calls=%fused_computation.24 | loop fusion | flops 25161728 | bytes 16846856 | tf_op jit(solution)/shard_map/reduce_sum | solution.py:118
  462.6 1.8 fusion.51
  464.4 0.7 copy-done.15
  465.1 1.7 fusion.57
  466.8 1.8 fusion.63
  468.6 1.8 fusion.69
  470.4 3.0 fusion.75
  473.4 2.8 fusion.81
  476.3 1.8 fusion.87
  478.1 1.8 fusion.99
  479.9 0.9 reshape_transpose_reshape.3
  (57 shorter events, 1.4 us)
Async XLA Ops:
  6.5 51.9 %copy-start = (bf16[7168,128]{1,0:T(8,128)(2,1)S(1)}, bf16[7168,128]{1,0:T(8,128)(2,1)}, u32[]{:S(2)}) copy-start(bf16[7168,128]{1,0:T(8,128)(2,1)} %param.12) | copy-start | bytes 5505028
  6.5 5.5 %copy-start.9 = (s32[2,128]{1,0:T(2,128)S(1)}, s32[2,128]{1,0:T(2,128)}, u32[]{:S(2)}) copy-start(s32[2,128]{1,0:T(2,128)} %param.19) | copy-start | bytes 3076
  6.5 51.9 %all-gather.2.cloned.1.call-start = ((), (), s32[]{:S(2)}) async-start(), calls=%async_computation | async-start | bytes 4128768 | tf_op jit(solution)/shard_map/all_gather | solution.py:66
  58.4 4.1 copy-start.2
  58.4 4.1 copy-start.4
  61.8 1.8 copy-start.3
  88.7 51.8 %collective-permute-start = (bf16[2,2,1,1024,128]{4,3,1,2,0:T(8,128)(2,1)S(1)}, bf16[2,2,1,1024,128]{4,3,1,2,0:T(8,128)(2,1)S(1)}, u32[]{:S(2)}, u32[]{:S(2)}) collective-permute-start(bf16[2,2,1,1024,128]{4,3,1,2,0:T(8,128)(2,1)S(1)} %pad_maximum_fusion), channel_id=1, source_target_pairs={{0,32},{8,40},{16,48},{24,56},{32,64},{40,72},{48,80},{56,88},{64,... | collective-permute-start | bytes 3145736 | tf_op jit(solution)/shard_map/ppermute | solution.py:23
  140.5 1.0 copy-start.10
  140.5 72.0 %collective-permute-start.1 = (bf16[2,2,1,1024,128]{4,3,1,2,0:T(8,128)(2,1)S(1)}, bf16[2,2,1,1024,128]{4,3,1,2,0:T(8,128)(2,1)S(1)}, u32[]{:S(2)}, u32[]{:S(2)}) collective-permute-start(bf16[2,2,1,1024,128]{4,3,1,2,0:T(8,128)(2,1)S(1)} %collective-permute-done), channel_id=1, source_target_pairs={{0,32},{8,40},{16,48},{24,56},{32,64},{40,72},{48,80},{56,88},{64,... | collective-permute-start | bytes 3145736 | tf_op jit(solution)/shard_map/ppermute | solution.py:23
  212.5 52.2 %copy-start.5 = (bf16[2,2,1,1024,128]{4,3,1,2,0:T(8,128)(2,1)}, bf16[2,2,1,1024,128]{4,3,1,2,0:T(8,128)(2,1)S(1)}, u32[]{:S(2)}) copy-start(bf16[2,2,1,1024,128]{4,3,1,2,0:T(8,128)(2,1)S(1)} %collective-permute-done.1) | copy-start | bytes 3145732
  212.5 52.2 %collective-permute-start.2 = (bf16[2,2,1,1024,128]{4,3,1,2,0:T(8,128)(2,1)S(1)}, bf16[2,2,1,1024,128]{4,3,1,2,0:T(8,128)(2,1)S(1)}, u32[]{:S(2)}, u32[]{:S(2)}) collective-permute-start(bf16[2,2,1,1024,128]{4,3,1,2,0:T(8,128)(2,1)S(1)} %collective-permute-done.1), channel_id=1, source_target_pairs={{0,32},{8,40},{16,48},{24,56},{32,64},{40,72},{48,80},{56,88},{64,... | collective-permute-start | bytes 3145736 | tf_op jit(solution)/shard_map/ppermute | solution.py:23
  264.7 71.8 %collective-permute-start.3 = (bf16[2,2,1,1024,128]{4,3,1,2,0:T(8,128)(2,1)S(1)}, bf16[2,2,1,1024,128]{4,3,1,2,0:T(8,128)(2,1)}, u32[]{:S(2)}, u32[]{:S(2)}) collective-permute-start(bf16[2,2,1,1024,128]{4,3,1,2,0:T(8,128)(2,1)S(1)} %collective-permute-done.2), channel_id=1, source_target_pairs={{0,32},{8,40},{16,48},{24,56},{32,64},{40,72},{48,80},{56,88},{64,... | collective-permute-start | bytes 3145736 | tf_op jit(solution)/shard_map/ppermute | solution.py:23
  336.5 50.7 %collective-permute-start.4 = (bf16[2,2,1,1024,128]{4,3,1,2,0:T(8,128)(2,1)}, bf16[2,2,1,1024,128]{4,3,1,2,0:T(8,128)(2,1)}, u32[]{:S(2)}, u32[]{:S(2)}) collective-permute-start(bf16[2,2,1,1024,128]{4,3,1,2,0:T(8,128)(2,1)} %collective-permute-done.3), channel_id=1, source_target_pairs={{0,32},{8,40},{16,48},{24,56},{32,64},{40,72},{48,80},{56,88},{64,... | collective-permute-start | bytes 3145736 | tf_op jit(solution)/shard_map/ppermute | solution.py:23
  342.9 44.2 %copy-start.6 = (bf16[2,2,1,1024,128]{4,3,1,2,0:T(8,128)(2,1)S(1)}, bf16[2,2,1,1024,128]{4,3,1,2,0:T(8,128)(2,1)}, u32[]{:S(2)}) copy-start(bf16[2,2,1,1024,128]{4,3,1,2,0:T(8,128)(2,1)} %copy-done.5) | copy-start | bytes 3145732
  345.0 71.9 %copy-start.13 = (f32[2,512,1024]{2,1,0:T(8,128)}, f32[2,512,1024]{2,1,0:T(8,128)S(1)}, u32[]{:S(2)}) copy-start(f32[2,512,1024]{2,1,0:T(8,128)S(1)} %get-tuple-element.69) | copy-start | bytes 12582916
  387.1 29.8 %collective-permute-start.5 = (bf16[2,2,1,1024,128]{4,3,1,2,0:T(8,128)(2,1)}, bf16[2,2,1,1024,128]{4,3,1,2,0:T(8,128)(2,1)S(1)}, u32[]{:S(2)}, u32[]{:S(2)}) collective-permute-start(bf16[2,2,1,1024,128]{4,3,1,2,0:T(8,128)(2,1)} %collective-permute-done.4), channel_id=1, source_target_pairs={{0,32},{8,40},{16,48},{24,56},{32,64},{40,72},{48,80},{56,88},{64,... | collective-permute-start | bytes 3145736 | tf_op jit(solution)/shard_map/ppermute | solution.py:23
  387.8 29.1 %copy-start.11 = (bf16[2,2,1,1024,128]{4,3,1,2,0:T(8,128)(2,1)S(1)}, bf16[2,2,1,1024,128]{4,3,1,2,0:T(8,128)(2,1)}, u32[]{:S(2)}) copy-start(bf16[2,2,1,1024,128]{4,3,1,2,0:T(8,128)(2,1)} %copy-done.10) | copy-start | bytes 3145732
  416.9 7.0 %copy-start.7 = (bf16[2,2,1,1024,128]{4,3,1,2,0:T(8,128)(2,1)}, bf16[2,2,1,1024,128]{4,3,1,2,0:T(8,128)(2,1)S(1)}, u32[]{:S(2)}) copy-start(bf16[2,2,1,1024,128]{4,3,1,2,0:T(8,128)(2,1)S(1)} %collective-permute-done.5) | copy-start | bytes 3145732
  416.9 28.7 %collective-permute-start.6 = (bf16[2,2,1,1024,128]{4,3,1,2,0:T(8,128)(2,1)S(1)}, bf16[2,2,1,1024,128]{4,3,1,2,0:T(8,128)(2,1)S(1)}, u32[]{:S(2)}, u32[]{:S(2)}) collective-permute-start(bf16[2,2,1,1024,128]{4,3,1,2,0:T(8,128)(2,1)S(1)} %collective-permute-done.5), channel_id=1, source_target_pairs={{0,32},{8,40},{16,48},{24,56},{32,64},{40,72},{48,80},{56,88},{64,... | collective-permute-start | bytes 3145736 | tf_op jit(solution)/shard_map/ppermute | solution.py:23
  456.1 6.5 %copy-start.14 = (f32[2,512,1024]{2,1,0:T(8,128)S(1)}, f32[2,512,1024]{2,1,0:T(8,128)}, u32[]{:S(2)}) copy-start(f32[2,512,1024]{2,1,0:T(8,128)} %copy-done.13) | copy-start | bytes 12582916
  462.5 1.8 copy-start.12
  462.6 2.5 copy-start.15
  473.4 2.8 copy-start.8
  478.1 2.7 copy-start.1
Sparse Core Ops, SparseCore 0:
  9.2 49.2 all-gather.1
where the time goes:
time: 488 us
  waiting for transfers between devices  379 us (78%)
  matrix products  48.1 us (10%)
  local copies, waits for them, and re-layouts  28.3 us (6%)
  other arithmetic  15 us (3%)
  between operations  14 us (3%)
    ppermute x7, waiting for transfers between devices, passed_along(): return lax.ppermute(value, axis, pairs)  332 us
    all_gather x1, waiting for transfers between devices, shards(): piece = lax.all_gather(hidden_sel, 'tp', axis=1, tiled=True)  46.3 us
    dot_general x8, matrix products, update(): jnp.einsum('bhqd,bhkd->bhqk', qblock, block[0], preferred_element_type=jn...  20.9 us
    dot_general x8, matrix products, update(): jnp.einsum('bhqk,bhkd->bhqd', weight.astype(jnp.bfloat16), block[1], pref...  16.5 us
    scatter x1, local copies, waits for them, and re-layouts, shards(): value_cache.reshape(slots, SPAN, heads, HD).at[slot_ids, sel_index]  12.5 us
    scatter x1, local copies, waits for them, and re-layouts, shards(): joined_key = cached.at[slot_ids, sel_index].set(new_key)  12.5 us
  transfers between devices with their start and end apart: 8, of which 8 were waited for; matrix products, arithmetic and copies ran while one was open for 5% of the time, Pallas kernels for 0%

commit v1 on v0

v1 whole, which is shorter than its diff:
```python
import math

import jax
import jax.numpy as jnp
from jax import lax
from jax.experimental import pallas as pl
from jax.experimental.pallas import tpu as pltpu
from jax.sharding import Mesh, PartitionSpec as P

HD = 128
HG = 4
R = 8
MAXCH = 8
SPAN = 1024
SEL = 128
SLOTS = 2
ROWS = SLOTS * SEL
QW = HG * HD
PACK = SEL + 16
DK = 896

rope_base = 5000000.0
low = -1.0e30
SCALE2 = math.log2(math.e) / math.sqrt(HD)

AXES = ("zh", "yh", "yp", "c", "zl", "x")


def px(v, s):
    return lax.ppermute(v, "x", [(i, (i + s) % 4) for i in range(4)])


def pz(v):
    return lax.ppermute(v, "zl", [(0, 1), (1, 0)])


def py(v):
    return lax.ppermute(v, "yh", [(0, 1), (1, 0)])


def ph(v, s):
    return lax.ppermute(v, "zh", [(i, (i + s) % 4) for i in range(4)])


def span_ranks(span_count, span_key):
    column = jnp.arange(MAXCH, dtype=jnp.int32)
    filled = column[None, :] < span_count[:, None]
    earlier = span_key[:, :, None] < span_key[:, None, :]
    ranks = jnp.sum((earlier & filled[:, :, None]).astype(jnp.int32), axis=1, dtype=jnp.int32)
    return filled.T.reshape(-1), ranks.T.reshape(-1)


def tables(position):
    freq = rope_base ** (-(jnp.arange(HD // 2, dtype=jnp.float32) * 2.0) / HD)
    angle = position.astype(jnp.float32)[:, None] * freq
    cosine, sine = jnp.cos(angle), jnp.sin(angle)
    return jnp.concatenate([cosine, cosine], -1), jnp.concatenate([-sine, sine], -1)


def turned(v, cosine, sine):
    return v * cosine + pltpu.roll(v, HD // 2, 1) * sine


def project_kernel(idx_ref, *refs):
    pieces = refs[:8]
    wq, wk, wv, cos_ref, sin_ref, q_ref, n_ref, acc_q, acc_n = refs[8:]
    k = pl.program_id(0)
    wn = jnp.concatenate([wk[...], wv[...]], axis=1)
    for i in range(8):

        @pl.when(k == i)
        def _(i=i):
            a = pieces[i][...]
            dq = jnp.dot(a, wq[...], preferred_element_type=jnp.float32)
            dn = jnp.dot(a, wn, preferred_element_type=jnp.float32)
            if i == 0:
                acc_q[...] = dq
                acc_n[...] = dn
            else:
                acc_q[...] += dq
                acc_n[...] += dn

    @pl.when(k == 7)
    def _():
        cosine, sine = cos_ref[...], sin_ref[...]
        for g in range(HG):
            at = slice(g * HD, (g + 1) * HD)
            q_ref[:, at] = turned(acc_q[:, at], cosine, sine).astype(jnp.bfloat16)
        n_ref[:ROWS, :] = turned(acc_n[:, :HD], cosine, sine).astype(jnp.bfloat16)
        n_ref[ROWS:, :] = acc_n[:, HD:].astype(jnp.bfloat16)


def project(idx, pieces, w_query, w_key, w_value, cosine, sine):
    full = lambda shape: pl.BlockSpec(shape, lambda k, idx: (0, 0))
    part = lambda width: pl.BlockSpec((DK, width), lambda k, idx: (idx[k], 0))
    return pl.pallas_call(
        project_kernel,
        out_shape=(
            jax.ShapeDtypeStruct((ROWS, QW), jnp.bfloat16),
            jax.ShapeDtypeStruct((2 * ROWS, HD), jnp.bfloat16),
        ),
        grid_spec=pltpu.PrefetchScalarGridSpec(
            num_scalar_prefetch=1,
            grid=(8,),
            in_specs=[full((ROWS, DK))] * 8
            + [part(QW), part(HD), part(HD), full((ROWS, HD)), full((ROWS, HD))],
            out_specs=(full((ROWS, QW)), full((2 * ROWS, HD))),
            scratch_shapes=[
                pltpu.VMEM((ROWS, QW), jnp.float32),
                pltpu.VMEM((ROWS, 2 * HD), jnp.float32),
            ],
        ),
        compiler_params=pltpu.CompilerParams(vmem_limit_bytes=32 << 20),
        cost_estimate=pl.CostEstimate(
            flops=2 * ROWS * 7168 * 768, bytes_accessed=15 << 20, transcendentals=0
        ),
        name="project",
    )(idx, *pieces, w_query, w_key, w_value, cosine, sine)


def attend_block(q, keys, vals, limit, m_ref, l_ref, acc_ref):
    s = lax.dot_general(q, keys, (((1,), (1,)), ((), ())), preferred_element_type=jnp.float32)
    if limit is not None:
        col = lax.broadcasted_iota(jnp.int32, s.shape, 1)
        s = jnp.where(col <= limit, s, low)
    old = m_ref[...]
    new = jnp.maximum(old, jnp.max(s, axis=1, keepdims=True))
    factor = jnp.exp2((old - new) * SCALE2)
    weight = jnp.exp2((s - new) * SCALE2)
    l_ref[...] = l_ref[...] * factor + jnp.sum(weight, axis=1, keepdims=True)
    acc_ref[...] = acc_ref[...] * factor + jnp.dot(
        weight.astype(jnp.bfloat16), vals, preferred_element_type=jnp.float32
    )
    m_ref[...] = new


def attend_source(own, r, q_ref, jk_ref, jv_ref, valid_ref, sel_ref, o_ref, m_ref, l_ref, acc_ref):
    m_ref[...] = jnp.full_like(m_ref, low)
    l_ref[...] = jnp.zeros_like(l_ref)
    acc_ref[...] = jnp.zeros_like(acc_ref)
    row = pl.multiple_of(r * SEL, SEL)

    def queries():
        q = q_ref[pl.ds(row, SEL), :]
        return jnp.concatenate([q[:, g * HD : (g + 1) * HD] for g in range(HG)], axis=0)

    for sp in range(2):

        @pl.when(valid_ref[r * 2 + sp] != 0)
        def _(sp=sp):
            limit = None
            if own and sp == 0:
                sel = sel_ref[pl.ds(row, SEL), :]
                limit = jnp.concatenate([sel] * HG, axis=0)
            attend_block(
                queries(), jk_ref[r * 2 + sp], jv_ref[r * 2 + sp], limit, m_ref, l_ref, acc_ref
            )

    l = l_ref[...]
    some = l > 0.0
    mixed = acc_ref[...] / jnp.where(some, l, 1.0)
    lse = jnp.where(some, m_ref[...] * SCALE2 + jnp.log2(jnp.where(some, l, 1.0)), low)
    lane = lax.broadcasted_iota(jnp.int32, (SEL, HD), 1)
    stat = jnp.zeros((SEL, HD), jnp.float32)
    for g in range(HG):
        o_ref[r, :SEL, g * HD : (g + 1) * HD] = mixed[g * SEL : (g + 1) * SEL].astype(jnp.bfloat16)
        rest = lse[g * SEL : (g + 1) * SEL]
        for k in range(3):
            part = rest.astype(jnp.bfloat16).astype(jnp.float32)
            stat = jnp.where(lane == k * HG + g, part, stat)
            rest = rest - part
    o_ref[r, SEL:, :HD] = stat.T[:16].astype(jnp.bfloat16)
    o_ref[r, SEL:, HD:] = jnp.zeros((16, QW - HD), jnp.bfloat16)


def own_kernel(
    valid_ref, q_ref, k0, v0, k1, v1, n0, n1, selr_ref, rot_ref, sel_ref,
    jk_ref, jv_ref, o_ref, m_ref, l_ref, acc_ref,
):
    def request(r, _):
        for sp, (kr, vr, nr) in enumerate(((k0, v0, n0), (k1, v1, n1))):
            base = pl.multiple_of(r * SPAN, SPAN)
            fresh = pl.multiple_of(r * SEL, SEL)
            raw = kr[pl.ds(base, SPAN), :].astype(jnp.float32)
            cached = turned(raw, rot_ref[r, sp : sp + 1, :], rot_ref[r, sp + 2 : sp + 3, :])
            at = lax.broadcasted_iota(jnp.int32, (SPAN, SEL), 0)
            pick = (at == selr_ref[r, sp : sp + 1, :]).astype(jnp.float32).astype(jnp.bfloat16)
            hit = jnp.dot(pick, jnp.ones((SEL, HD), jnp.bfloat16), preferred_element_type=jnp.float32)
            hit = hit > 0.5
            put_k = jnp.dot(pick, nr[pl.ds(fresh, SEL), :], preferred_element_type=jnp.float32)
            put_v = jnp.dot(
                pick, nr[pl.ds(ROWS + fresh, SEL), :], preferred_element_type=jnp.float32
            )
            jk_ref[r * 2 + sp] = jnp.where(hit, put_k, cached).astype(jnp.bfloat16)
            vals = vr[pl.ds(base, SPAN), :].astype(jnp.float32)
            jv_ref[r * 2 + sp] = jnp.where(hit, put_v, vals).astype(jnp.bfloat16)
        attend_source(
            True, r, q_ref, jk_ref, jv_ref, valid_ref, sel_ref, o_ref, m_ref, l_ref, acc_ref
        )
        return 0

    lax.fori_loop(0, SLOTS, request, 0)


def other_kernel(valid_ref, q_ref, jk_ref, jv_ref, o_ref, m_ref, l_ref, acc_ref):
    def request(r, _):
        attend_source(
            False, r, q_ref, jk_ref, jv_ref, valid_ref, None, o_ref, m_ref, l_ref, acc_ref
        )
        return 0

    lax.fori_loop(0, SLOTS, request, 0)


vmem = pl.BlockSpec(memory_space=pltpu.VMEM)
smem = pl.BlockSpec(memory_space=pltpu.SMEM)
joined_shape = jax.ShapeDtypeStruct((SLOTS * 2, SPAN, HD), jnp.bfloat16)
packed_shape = jax.ShapeDtypeStruct((SLOTS, PACK, QW), jnp.bfloat16)
state_scratch = [
    pltpu.VMEM((HG * SEL, 1), jnp.float32),
    pltpu.VMEM((HG * SEL, 1), jnp.float32),
    pltpu.VMEM((HG * SEL, HD), jnp.float32),
]
attend_cost = pl.CostEstimate(
    flops=4 * SLOTS * 512 * 1024 * HD * 2, bytes_accessed=3 << 20, transcendentals=2 << 20
)


def attend_own(*args):
    return pl.pallas_call(
        own_kernel,
        out_shape=(joined_shape, joined_shape, packed_shape),
        in_specs=[smem] + [vmem] * 10,
        out_specs=(vmem, vmem, vmem),
        scratch_shapes=state_scratch,
        compiler_params=pltpu.CompilerParams(vmem_limit_bytes=32 << 20),
        cost_estimate=attend_cost,
        name="attend_own",
    )(*args)


def attend_other(*args):
    return pl.pallas_call(
        other_kernel,
        out_shape=packed_shape,
        in_specs=[smem] + [vmem] * 3,
        out_specs=vmem,
        scratch_shapes=state_scratch,
        compiler_params=pltpu.CompilerParams(vmem_limit_bytes=32 << 20),
        cost_estimate=attend_cost,
        name="attend_other",
    )(*args)


def merge_kernel(a, b, c, d, o_ref):
    parts = (a, b, c, d)
    for r in range(SLOTS):
        lse = []
        for p in parts:
            stat = p[r, SEL:, :HD].astype(jnp.float32)
            full = stat[0:4] + stat[4:8] + stat[8:12]
            lse.append(jnp.concatenate([full, jnp.zeros((HD - 4, SEL), jnp.float32)], axis=0).T)
        top = jnp.maximum(jnp.maximum(lse[0], lse[1]), jnp.maximum(lse[2], lse[3]))
        weight = [jnp.exp2(v - top) for v in lse]
        total = weight[0] + weight[1] + weight[2] + weight[3]
        weight = [w / total for w in weight]
        for g in range(HG):
            at = slice(g * HD, (g + 1) * HD)
            mixed = jnp.zeros((SEL, HD), jnp.float32)
            for w, p in zip(weight, parts):
                mixed += w[:, g : g + 1] * p[r, :SEL, at].astype(jnp.float32)
            o_ref[r * SEL : (r + 1) * SEL, at] = mixed.astype(jnp.bfloat16)


def merge(*parts):
    return pl.pallas_call(
        merge_kernel,
        out_shape=jax.ShapeDtypeStruct((ROWS, QW), jnp.bfloat16),
        in_specs=[vmem] * 4,
        out_specs=vmem,
        compiler_params=pltpu.CompilerParams(vmem_limit_bytes=16 << 20),
        name="merge",
    )(*parts)


def shards(
    hidden, w_query, w_key, w_value, key_cache, value_cache,
    span_count, span_key, cache_offset, sel_index,
):
    zh, yh, yp, c = (lax.axis_index(a) for a in ("zh", "yh", "yp", "c"))
    zl, x = lax.axis_index("zl"), lax.axis_index("x")
    z = pz(hidden)
    k1, v1 = py(key_cache), py(value_cache)
    mine = jnp.concatenate(
        [sel_index, jnp.broadcast_to(cache_offset[:, None], (SLOTS, SEL))], axis=0
    )
    theirs = py(mine)
    right, left = px(hidden, 1), px(hidden, -1)
    zright, zleft = px(z, 1), px(z, -1)
    far, zfar = px(right, 1), px(zleft, -1)
    pieces = (hidden, z, right, left, zright, zleft, far, zfar)
    other = 1 - zl
    idx = jnp.stack(
        [
            zl * 4 + x,
            other * 4 + x,
            zl * 4 + (x + 3) % 4,
            zl * 4 + (x + 1) % 4,
            other * 4 + (x + 3) % 4,
            other * 4 + (x + 1) % 4,
            zl * 4 + (x + 2) % 4,
            other * 4 + (x + 2) % 4,
        ]
    ).astype(jnp.int32)

    filled_all, rank_all = span_ranks(span_count, span_key)

    def first_slot(h, half):
        return (((h * 2 + half) * 2 + yp) * 2 + c) * SLOTS

    def lookup(h, half):
        start = first_slot(h, half)
        return (
            lax.dynamic_slice_in_dim(filled_all, start, SLOTS),
            lax.dynamic_slice_in_dim(rank_all, start, SLOTS),
        )

    span_f, span_r = zip(lookup(zh, yh), lookup(zh, 1 - yh))

    def validity(shift):
        qf, qr = lookup((zh - shift) % 4, yh)
        table = [qf & kf & (kr <= qr) for kf, kr in zip(span_f, span_r)]
        return jnp.stack(table, axis=1).reshape(-1).astype(jnp.int32)

    position = (span_r[0][:, None] * SPAN + sel_index).reshape(-1)
    cosine, sine = tables(position)
    delta = jnp.stack(
        [span_r[0] * SPAN - cache_offset, span_r[1] * SPAN - theirs[SLOTS:, 0]], axis=1
    ).reshape(-1)
    turn_c, turn_s = tables(delta)
    rot = jnp.concatenate(
        [turn_c.reshape(SLOTS, 2, HD), turn_s.reshape(SLOTS, 2, HD)], axis=1
    )
    sel_rows = jnp.stack([sel_index, theirs[:SLOTS]], axis=1)

    query, fresh = project(idx, pieces, w_query, w_key, w_value, cosine, sine)
    fresh1 = py(fresh)
    sent = {s: ph(query, s) for s in (2, 1, 3)}
    jk, jv, part0 = attend_own(
        validity(0), query, key_cache, value_cache, k1, v1, fresh, fresh1,
        sel_rows, rot, sel_index.reshape(ROWS, 1),
    )
    back = [ph(attend_other(validity(s), sent[s], jk, jv), -s) for s in (1, 3, 2)]
    return merge(part0, *back)


def solution(mesh):
    split = Mesh(mesh.devices.reshape(4, 2, 2, 2, 2, 4), AXES)
    seq, tp = AXES[:4], AXES[4:]
    placed = (
        P(seq, tp),
        P(None, tp),
        P(None, tp),
        P(None, tp),
        P(seq, tp),
        P(seq, tp),
        P(),
        P(),
        P(seq),
        P(seq, None),
    )
    return jax.shard_map(
        shards, mesh=split, in_specs=placed, out_specs=P(seq, tp), check_vma=False
    )
```

time: 488 us -> 115 us (0.24)
  the two profiles are of different devices: /device:TPU:132 before, /device:TPU:32 now
where the time goes in v1:
time: 115 us; the launch traced here: 116 us
  starting transfers between devices  40.4 us (35%)
  waiting for transfers between devices  35.6 us (31%)
  Pallas kernels  25 us (22%)
  local copies, waits for them, and re-layouts  9.54 us (8%)
  other arithmetic  4.92 us (4%)
    ppermute x6, waiting for transfers between devices, ph(): return lax.ppermute(v, 'zh', [(i, (i + s) % 4) for i in range(4)])  21.9 us
    ppermute x6, starting transfers between devices, ph(): return lax.ppermute(v, 'zh', [(i, (i + s) % 4) for i in range(4)])  19.1 us
    ppermute x6, waiting for transfers between devices, px(): return lax.ppermute(v, 'x', [(i, (i + s) % 4) for i in range(4)])  13.8 us
    ppermute x4, starting transfers between devices, py(): return lax.ppermute(v, 'yh', [(0, 1), (1, 0)])  10.2 us
    pallas_call x3, Pallas kernels, attend_other(): pl.pallas_call(other_kernel, out_shape=packed_shape, in_specs=[smem] + [v...  9.32 us
    ppermute x6, starting transfers between devices, px(): return lax.ppermute(v, 'x', [(i, (i + s) % 4) for i in range(4)])  9.2 us
    pallas_call x1, Pallas kernels, attend_own(): pl.pallas_call(own_kernel, out_shape=(joined_shape, joined_shape, packed_...  7.28 us
    pallas_call x1, Pallas kernels, project(): pl.pallas_call(project_kernel, out_shape=(jax.ShapeDtypeStruct((ROWS, QW)...  6.86 us
  transfers between devices with their start and end apart: 17, of which 6 were waited for; matrix products, arithmetic and copies ran while one was open for 7% of the time, Pallas kernels for 20%

profile of v1, /device:TPU:32, one launch (start us, length us, event | category | flops | bytes accessed | tf_op | source)
XLA Modules:
  0.0 115.6 jit_solution(3954881489965004345)
XLA Ops:
  0.0 1.8 %collective-permute-start = (bf16[256,896]{1,0:T(8,128)(2,1)}, bf16[256,896]{1,0:T(8,128)(2,1)S(1)}, u32[]{:S(2)}, u32[]{:S(2)}) collective-permute-start(bf16[256,896]{1,0:T(8,128)(2,1)} %refs_0_.1), channel_id=1, source_target_pairs={{0,4},{4,0},{1,5},{5,1},{2,6},{6,2},{3,7},{7,3},{8,12},{12,8},{9,1... | collective-permute-start | bytes 1376264 | tf_op jit(solution)/shard_map/ppermute | solution.py:34
  1.9 3.2 %collective-permute-start.2 = (bf16[256,896]{1,0:T(8,128)(2,1)}, bf16[256,896]{1,0:T(8,128)(2,1)S(1)}, u32[]{:S(2)}, u32[]{:S(2)}) collective-permute-start(bf16[256,896]{1,0:T(8,128)(2,1)} %refs_0_.1), channel_id=1, source_target_pairs={{0,3},{1,0},{2,1},{3,2},{4,7},{5,4},{6,5},{7,6},{8,11},{9,8},{10,9... | collective-permute-start | bytes 1376264 | tf_op jit(solution)/shard_map/ppermute | solution.py:30
  5.1 0.7 pad.15.clone
  5.8 0.7 pad_add_fusion
  6.6 1.5 %collective-permute-start.10 = (s32[4,128]{1,0:T(4,128)S(1)}, s32[4,128]{1,0:T(4,128)S(1)}, u32[]{:S(2)}, u32[]{:S(2)}) collective-permute-start(s32[4,128]{1,0:T(4,128)S(1)} %pad_add_fusion), channel_id=1, source_target_pairs={{0,32},{32,0},{1,33},{33,1},{2,34},{34,2},{3,35},{35,3},{4,36},{36... | collective-permute-start | bytes 6152 | tf_op jit(solution)/shard_map/ppermute | solution.py:38
  8.0 2.1 %collective-permute-start.7 = (bf16[2048,128]{1,0:T(8,128)(2,1)}, bf16[2048,128]{1,0:T(8,128)(2,1)}, u32[]{:S(2)}, u32[]{:S(2)}) collective-permute-start(bf16[2048,128]{1,0:T(8,128)(2,1)} %k0.1), channel_id=1, source_target_pairs={{0,32},{32,0},{1,33},{33,1},{2,34},{34,2},{3,35},{35,3},{4,36},{36... | collective-permute-start | bytes 1572872 | tf_op jit(solution)/shard_map/ppermute | solution.py:38
  10.1 0.8 iota_compare_fusion
  10.9 0.9 convert_reduce_fusion
  11.9 0.1 lt.104
  12.0 0.1 and_bitcast_fusion.1
  12.1 0.7 subtract_bitcast_fusion.1
  12.9 0.8 convert_bitcast_fusion
  13.6 0.5 fusion
  14.2 1.1 collective-permute-start.4
  15.2 0.1 pad_maximum_fusion
  15.4 0.1 copy.23
  15.6 1.5 %copy.25.sel_ref = s32[256,1]{1,0:T(8,128)} copy(s32[256,1]{0,1:T(1,128)} %bitcast.34) | data formatting | bytes 2048 | tf_op jit(solution)/shard_map/reshape | solution.py:351
  17.1 0.1 copy.28
  17.3 0.1 copy.27
  17.4 0.1 copy.26
  17.7 0.1 slice_reduce_fusion
  17.8 1.1 collective-permute-start.3
  18.9 0.1 collective-permute-start.5
  19.0 5.1 %collective-permute-done.4.refs_5_ = bf16[256,896]{1,0:T(8,128)(2,1)S(1)} collective-permute-done((bf16[256,896]{1,0:T(8,128)(2,1)S(1)}, bf16[256,896]{1,0:T(8,128)(2,1)S(1)}, u32[]{:S(2)}, u32[]{:S(2)}) %collective-permute-start.4) | collective-permute-done | bytes 458784 | tf_op jit(solution)/shard_map/ppermute | solution.py:30
  24.1 3.7 %collective-permute-start.6 = (bf16[256,896]{1,0:T(8,128)(2,1)S(1)}, bf16[256,896]{1,0:T(8,128)(2,1)}, u32[]{:S(2)}, u32[]{:S(2)}) collective-permute-start(bf16[256,896]{1,0:T(8,128)(2,1)S(1)} %collective-permute-done.4.refs_5_), channel_id=1, source_target_pairs={{0,3},{1,0},{2,1},{3,2},{4,7},{5,4},{6,5},{7,6},{8,11},{9,8},{10,9... | collective-permute-start | bytes 1376264 | tf_op jit(solution)/shard_map/ppermute | solution.py:30
  27.8 0.1 copy.24
  27.9 3.3 %collective-permute-start.8 = (bf16[2048,128]{1,0:T(8,128)(2,1)}, bf16[2048,128]{1,0:T(8,128)(2,1)S(1)}, u32[]{:S(2)}, u32[]{:S(2)}) collective-permute-start(bf16[2048,128]{1,0:T(8,128)(2,1)} %v0.1), channel_id=1, source_target_pairs={{0,32},{32,0},{1,33},{33,1},{2,34},{34,2},{3,35},{35,3},{4,36},{36... | collective-permute-start | bytes 1572872 | tf_op jit(solution)/shard_map/ppermute | solution.py:38
  31.3 0.1 multiply_cosine_fusion.1
  31.4 1.2 %collective-permute-done.3.refs_4_ = bf16[256,896]{1,0:T(8,128)(2,1)S(1)} collective-permute-done((bf16[256,896]{1,0:T(8,128)(2,1)S(1)}, bf16[256,896]{1,0:T(8,128)(2,1)S(1)}, u32[]{:S(2)}, u32[]{:S(2)}) %collective-permute-start.3) | collective-permute-done | bytes 458784 | tf_op jit(solution)/shard_map/ppermute | solution.py:30
  32.6 7.5 %collective-permute-done.5.refs_6_ = bf16[256,896]{1,0:T(8,128)(2,1)S(1)} collective-permute-done((bf16[256,896]{1,0:T(8,128)(2,1)S(1)}, bf16[256,896]{1,0:T(8,128)(2,1)S(1)}, u32[]{:S(2)}, u32[]{:S(2)}) %collective-permute-start.5) | collective-permute-done | bytes 458784 | tf_op jit(solution)/shard_map/ppermute | solution.py:30
  40.1 3.1 %copy-done = bf16[7168,512]{1,0:T(8,128)(2,1)S(1)} copy-done((bf16[7168,512]{1,0:T(8,128)(2,1)S(1)}, bf16[7168,512]{1,0:T(8,128)(2,1)}, u32[]{:S(2)}) %copy-start) | copy-done | bytes 7340056
  43.1 1.5 %copy-done.1 = bf16[7168,128]{1,0:T(8,128)(2,1)S(1)} copy-done((bf16[7168,128]{1,0:T(8,128)(2,1)S(1)}, bf16[7168,128]{1,0:T(8,128)(2,1)}, u32[]{:S(2)}) %copy-start.1) | copy-done | bytes 1835032
  44.6 1.5 %copy-done.2 = bf16[7168,128]{1,0:T(8,128)(2,1)S(1)} copy-done((bf16[7168,128]{1,0:T(8,128)(2,1)S(1)}, bf16[7168,128]{1,0:T(8,128)(2,1)}, u32[]{:S(2)}) %copy-start.2) | copy-done | bytes 1835032
  46.1 6.9 %project.1 = (bf16[256,512]{1,0:T(8,128)(2,1)S(1)}, bf16[512,128]{1,0:T(8,128)(2,1)S(1)}) custom-call(s32[8]{0:T(128)S(1)} %stack.92.idx_ref, bf16[256,896]{1,0:T(8,128)(2,1)S(1)} %copy-done.3, bf16[256,896]{1,0:T(8,128)(2,1)S(1)} %collective-permute-done.refs_1_, bf16[256,896]{1,0:T(8,128)(2,1)S(1)} %collective-permute-done.1.refs_2_, ...), custom_call_target="tpu_custom_call" | custom-call | flops 2818572288 | bytes 15728640 | tf_op jit(solution)/shard_map/project/pallas_call | solution.py:96
  53.0 3.4 %collective-permute-start.9 = (bf16[512,128]{1,0:T(8,128)(2,1)S(1)}, bf16[512,128]{1,0:T(8,128)(2,1)S(1)}, u32[]{:S(2)}, u32[]{:S(2)}) collective-permute-start(bf16[512,128]{1,0:T(8,128)(2,1)S(1)} %get-tuple-element.11.n0), channel_id=1, source_target_pairs={{0,32},{32,0},{1,33},{33,1},{2,34},{34,2},{3,35},{35,3},{4,36},{36... | collective-permute-start | bytes 393224 | tf_op jit(solution)/shard_map/ppermute | solution.py:38
  56.4 6.3 %collective-permute-start.15 = (bf16[256,512]{1,0:T(8,128)(2,1)S(1)}, bf16[256,512]{1,0:T(8,128)(2,1)S(1)}, u32[]{:S(2)}, u32[]{:S(2)}) collective-permute-start(bf16[256,512]{1,0:T(8,128)(2,1)S(1)} %get-tuple-element.10.q_ref), channel_id=1, source_target_pairs={{0,128},{64,192},{128,0},{192,64},{1,129},{65,193},{129,1},{193,65... | collective-permute-start | bytes 786440 | tf_op jit(solution)/shard_map/ppermute | solution.py:42
  62.8 0.6 collective-permute-start.13
  63.4 2.5 %collective-permute-start.11 = (bf16[256,512]{1,0:T(8,128)(2,1)S(1)}, bf16[256,512]{1,0:T(8,128)(2,1)S(1)}, u32[]{:S(2)}, u32[]{:S(2)}) collective-permute-start(bf16[256,512]{1,0:T(8,128)(2,1)S(1)} %get-tuple-element.10.q_ref), channel_id=1, source_target_pairs={{0,64},{64,128},{128,192},{192,0},{1,65},{65,129},{129,193},{193,1... | collective-permute-start | bytes 786440 | tf_op jit(solution)/shard_map/ppermute | solution.py:42
  65.9 7.3 %attend_own.1 = (bf16[4,1024,128]{2,1,0:T(8,128)(2,1)S(1)}, bf16[4,1024,128]{2,1,0:T(8,128)(2,1)S(1)}, bf16[2,144,512]{2,1,0:T(8,128)(2,1)S(1)}) custom-call(s32[4]{0:T(128)S(1)} %reshape.114.valid_ref, bf16[256,512]{1,0:T(8,128)(2,1)S(1)} %get-tuple-element.10.q_ref, bf16[2048,128]{1,0:T(8,128)(2,1)S(1)} %copy-done.5, bf16[2048,128]{1,0:T(8,128)(2,1)S(1)} %copy-done.6, ...), custom_call_target="tpu_custom_call" | custom-call | flops 1073741824 | bytes 3145728 | tf_op jit(solution)/shard_map/attend_own/pallas_call | solution.py:230
  73.1 1.3 %collective-permute-done.15.q_ref = bf16[256,512]{1,0:T(8,128)(2,1)S(1)} collective-permute-done((bf16[256,512]{1,0:T(8,128)(2,1)S(1)}, bf16[256,512]{1,0:T(8,128)(2,1)S(1)}, u32[]{:S(2)}, u32[]{:S(2)}) %collective-permute-start.15) | collective-permute-done | bytes 262176 | tf_op jit(solution)/shard_map/ppermute | solution.py:42
  74.4 1.3 %attend_other.5 = bf16[2,144,512]{2,1,0:T(8,128)(2,1)S(1)} custom-call(s32[4]{0:T(128)S(1)} %reshape.117.valid_ref, bf16[256,512]{1,0:T(8,128)(2,1)S(1)} %collective-permute-done.15.q_ref, bf16[4,1024,128]{2,1,0:T(8,128)(2,1)S(1)} %get-tuple-element.13.jk_ref, bf16[4,1024,128]{2,1,0:T(8,128)(2,1)S(1)} %get-tuple-element.14.jv_ref), custom_call_target="tpu_custom_call" | custom-call | flops 1073741824 | bytes 3145728 | tf_op jit(solution)/shard_map/attend_other/pallas_call | solution.py:243
  75.7 5.6 %collective-permute-start.16 = (bf16[2,144,512]{2,1,0:T(8,128)(2,1)S(1)}, bf16[2,144,512]{2,1,0:T(8,128)(2,1)S(1)}, u32[]{:S(2)}, u32[]{:S(2)}) collective-permute-start(bf16[2,144,512]{2,1,0:T(8,128)(2,1)S(1)} %attend_other.5), channel_id=1, source_target_pairs={{0,128},{64,192},{128,0},{192,64},{1,129},{65,193},{129,1},{193,65... | collective-permute-start | bytes 884744 | tf_op jit(solution)/shard_map/ppermute | solution.py:42
  81.2 9.0 %collective-permute-done.13.q_ref = bf16[256,512]{1,0:T(8,128)(2,1)S(1)} collective-permute-done((bf16[256,512]{1,0:T(8,128)(2,1)S(1)}, bf16[256,512]{1,0:T(8,128)(2,1)S(1)}, u32[]{:S(2)}, u32[]{:S(2)}) %collective-permute-start.13) | collective-permute-done | bytes 262176 | tf_op jit(solution)/shard_map/ppermute | solution.py:42
  90.3 6.8 %attend_other.4 = bf16[2,144,512]{2,1,0:T(8,128)(2,1)S(1)} custom-call(s32[4]{0:T(128)S(1)} %reshape.116.valid_ref, bf16[256,512]{1,0:T(8,128)(2,1)S(1)} %collective-permute-done.13.q_ref, bf16[4,1024,128]{2,1,0:T(8,128)(2,1)S(1)} %get-tuple-element.13.jk_ref, bf16[4,1024,128]{2,1,0:T(8,128)(2,1)S(1)} %get-tuple-element.14.jv_ref), custom_call_target="tpu_custom_call" | custom-call | flops 1073741824 | bytes 3145728 | tf_op jit(solution)/shard_map/attend_other/pallas_call | solution.py:243
  97.1 1.3 %attend_other.3 = bf16[2,144,512]{2,1,0:T(8,128)(2,1)S(1)} custom-call(s32[4]{0:T(128)S(1)} %reshape.115.valid_ref, bf16[256,512]{1,0:T(8,128)(2,1)S(1)} %collective-permute-done.11.q_ref, bf16[4,1024,128]{2,1,0:T(8,128)(2,1)S(1)} %get-tuple-element.13.jk_ref, bf16[4,1024,128]{2,1,0:T(8,128)(2,1)S(1)} %get-tuple-element.14.jv_ref), custom_call_target="tpu_custom_call" | custom-call | flops 1073741824 | bytes 3145728 | tf_op jit(solution)/shard_map/attend_other/pallas_call | solution.py:243
  98.4 4.2 %collective-permute-start.12 = (bf16[2,144,512]{2,1,0:T(8,128)(2,1)S(1)}, bf16[2,144,512]{2,1,0:T(8,128)(2,1)S(1)}, u32[]{:S(2)}, u32[]{:S(2)}) collective-permute-start(bf16[2,144,512]{2,1,0:T(8,128)(2,1)S(1)} %attend_other.3), channel_id=1, source_target_pairs={{0,192},{64,0},{128,64},{192,128},{1,193},{65,1},{129,65},{193,129... | collective-permute-start | bytes 884744 | tf_op jit(solution)/shard_map/ppermute | solution.py:42
  102.6 11.5 %collective-permute-done.14.c = bf16[2,144,512]{2,1,0:T(8,128)(2,1)S(1)} collective-permute-done((bf16[2,144,512]{2,1,0:T(8,128)(2,1)S(1)}, bf16[2,144,512]{2,1,0:T(8,128)(2,1)S(1)}, u32[]{:S(2)}, u32[]{:S(2)}) %collective-permute-start.14) | collective-permute-done | bytes 294944 | tf_op jit(solution)/shard_map/ppermute | solution.py:42
  114.1 1.5 %merge.1 = bf16[256,512]{1,0:T(8,128)(2,1)} custom-call(bf16[2,144,512]{2,1,0:T(8,128)(2,1)S(1)} %get-tuple-element.12.a, bf16[2,144,512]{2,1,0:T(8,128)(2,1)S(1)} %collective-permute-done.12.b, bf16[2,144,512]{2,1,0:T(8,128)(2,1)S(1)} %collective-permute-done.14.c, bf16[2,144,512]{2,1,0:T(8,128)(2,1)S(1)} %collective-permute-done.16.d), custom_call_target="tpu_custom_call" | custom-call | tf_op jit(solution)/shard_map/merge/pallas_call | solution.py:276
  (43 shorter events, 0.9 us)
Async XLA Ops:
  0.0 40.0 %copy-start.3 = (bf16[256,896]{1,0:T(8,128)(2,1)S(1)}, bf16[256,896]{1,0:T(8,128)(2,1)}, u32[]{:S(2)}) copy-start(bf16[256,896]{1,0:T(8,128)(2,1)} %refs_0_.1) | copy-start | bytes 1376260
  0.0 14.2 %collective-permute-start = (bf16[256,896]{1,0:T(8,128)(2,1)}, bf16[256,896]{1,0:T(8,128)(2,1)S(1)}, u32[]{:S(2)}, u32[]{:S(2)}) collective-permute-start(bf16[256,896]{1,0:T(8,128)(2,1)} %refs_0_.1), channel_id=1, source_target_pairs={{0,4},{4,0},{1,5},{5,1},{2,6},{6,2},{3,7},{7,3},{8,12},{12,8},{9,1... | collective-permute-start | bytes 1376264 | tf_op jit(solution)/shard_map/ppermute | solution.py:34
  1.8 17.1 %collective-permute-start.1 = (bf16[256,896]{1,0:T(8,128)(2,1)}, bf16[256,896]{1,0:T(8,128)(2,1)S(1)}, u32[]{:S(2)}, u32[]{:S(2)}) collective-permute-start(bf16[256,896]{1,0:T(8,128)(2,1)} %refs_0_.1), channel_id=1, source_target_pairs={{0,1},{1,2},{2,3},{3,0},{4,5},{5,6},{6,7},{7,4},{8,9},{9,10},{10,1... | collective-permute-start | bytes 1376264 | tf_op jit(solution)/shard_map/ppermute | solution.py:30
  1.9 26.1 %collective-permute-start.2 = (bf16[256,896]{1,0:T(8,128)(2,1)}, bf16[256,896]{1,0:T(8,128)(2,1)S(1)}, u32[]{:S(2)}, u32[]{:S(2)}) collective-permute-start(bf16[256,896]{1,0:T(8,128)(2,1)} %refs_0_.1), channel_id=1, source_target_pairs={{0,3},{1,0},{2,1},{3,2},{4,7},{5,4},{6,5},{7,6},{8,11},{9,8},{10,9... | collective-permute-start | bytes 1376264 | tf_op jit(solution)/shard_map/ppermute | solution.py:30
  6.6 11.1 %collective-permute-start.10 = (s32[4,128]{1,0:T(4,128)S(1)}, s32[4,128]{1,0:T(4,128)S(1)}, u32[]{:S(2)}, u32[]{:S(2)}) collective-permute-start(s32[4,128]{1,0:T(4,128)S(1)} %pad_add_fusion), channel_id=1, source_target_pairs={{0,32},{32,0},{1,33},{33,1},{2,34},{34,2},{3,35},{35,3},{4,36},{36... | collective-permute-start | bytes 6152 | tf_op jit(solution)/shard_map/ppermute | solution.py:38
  8.0 55.3 %collective-permute-start.7 = (bf16[2048,128]{1,0:T(8,128)(2,1)}, bf16[2048,128]{1,0:T(8,128)(2,1)}, u32[]{:S(2)}, u32[]{:S(2)}) collective-permute-start(bf16[2048,128]{1,0:T(8,128)(2,1)} %k0.1), channel_id=1, source_target_pairs={{0,32},{32,0},{1,33},{33,1},{2,34},{34,2},{3,35},{35,3},{4,36},{36... | collective-permute-start | bytes 1572872 | tf_op jit(solution)/shard_map/ppermute | solution.py:38
  14.2 10.0 %collective-permute-start.4 = (bf16[256,896]{1,0:T(8,128)(2,1)S(1)}, bf16[256,896]{1,0:T(8,128)(2,1)S(1)}, u32[]{:S(2)}, u32[]{:S(2)}) collective-permute-start(bf16[256,896]{1,0:T(8,128)(2,1)S(1)} %collective-permute-done.refs_1_), channel_id=1, source_target_pairs={{0,3},{1,0},{2,1},{3,2},{4,7},{5,4},{6,5},{7,6},{8,11},{9,8},{10,9... | collective-permute-start | bytes 1376264 | tf_op jit(solution)/shard_map/ppermute | solution.py:30
  17.8 14.7 %collective-permute-start.3 = (bf16[256,896]{1,0:T(8,128)(2,1)S(1)}, bf16[256,896]{1,0:T(8,128)(2,1)S(1)}, u32[]{:S(2)}, u32[]{:S(2)}) collective-permute-start(bf16[256,896]{1,0:T(8,128)(2,1)S(1)} %collective-permute-done.refs_1_), channel_id=1, source_target_pairs={{0,1},{1,2},{2,3},{3,0},{4,5},{5,6},{6,7},{7,4},{8,9},{9,10},{10,1... | collective-permute-start | bytes 1376264 | tf_op jit(solution)/shard_map/ppermute | solution.py:30
  18.9 21.1 %collective-permute-start.5 = (bf16[256,896]{1,0:T(8,128)(2,1)S(1)}, bf16[256,896]{1,0:T(8,128)(2,1)S(1)}, u32[]{:S(2)}, u32[]{:S(2)}) collective-permute-start(bf16[256,896]{1,0:T(8,128)(2,1)S(1)} %collective-permute-done.1.refs_2_), channel_id=1, source_target_pairs={{0,1},{1,2},{2,3},{3,0},{4,5},{5,6},{6,7},{7,4},{8,9},{9,10},{10,1... | collective-permute-start | bytes 1376264 | tf_op jit(solution)/shard_map/ppermute | solution.py:30
  24.1 15.9 %collective-permute-start.6 = (bf16[256,896]{1,0:T(8,128)(2,1)S(1)}, bf16[256,896]{1,0:T(8,128)(2,1)}, u32[]{:S(2)}, u32[]{:S(2)}) collective-permute-start(bf16[256,896]{1,0:T(8,128)(2,1)S(1)} %collective-permute-done.4.refs_5_), channel_id=1, source_target_pairs={{0,3},{1,0},{2,1},{3,2},{4,7},{5,4},{6,5},{7,6},{8,11},{9,8},{10,9... | collective-permute-start | bytes 1376264 | tf_op jit(solution)/shard_map/ppermute | solution.py:30
  27.9 37.9 %collective-permute-start.8 = (bf16[2048,128]{1,0:T(8,128)(2,1)}, bf16[2048,128]{1,0:T(8,128)(2,1)S(1)}, u32[]{:S(2)}, u32[]{:S(2)}) collective-permute-start(bf16[2048,128]{1,0:T(8,128)(2,1)} %v0.1), channel_id=1, source_target_pairs={{0,32},{32,0},{1,33},{33,1},{2,34},{34,2},{3,35},{35,3},{4,36},{36... | collective-permute-start | bytes 1572872 | tf_op jit(solution)/shard_map/ppermute | solution.py:38
  40.0 3.1 %copy-start = (bf16[7168,512]{1,0:T(8,128)(2,1)S(1)}, bf16[7168,512]{1,0:T(8,128)(2,1)}, u32[]{:S(2)}) copy-start(bf16[7168,512]{1,0:T(8,128)(2,1)} %refs_8_.1) | copy-start | bytes 22020100
  43.1 1.5 %copy-start.1 = (bf16[7168,128]{1,0:T(8,128)(2,1)S(1)}, bf16[7168,128]{1,0:T(8,128)(2,1)}, u32[]{:S(2)}) copy-start(bf16[7168,128]{1,0:T(8,128)(2,1)} %refs_9_.1) | copy-start | bytes 5505028
  44.6 1.5 %copy-start.2 = (bf16[7168,128]{1,0:T(8,128)(2,1)S(1)}, bf16[7168,128]{1,0:T(8,128)(2,1)}, u32[]{:S(2)}) copy-start(bf16[7168,128]{1,0:T(8,128)(2,1)} %refs_10_.1) | copy-start | bytes 5505028
  46.1 17.2 %copy-start.7 = (s32[2,128]{1,0:T(2,128)S(1)}, s32[2,128]{1,0:T(2,128)}, u32[]{:S(2)}) copy-start(s32[2,128]{1,0:T(2,128)} %param.19) | copy-start | bytes 3076
  46.1 19.7 %copy-start.4 = (s32[256,1]{1,0:T(8,128)S(1)}, s32[256,1]{1,0:T(8,128)}, u32[]{:S(2)}) copy-start(s32[256,1]{1,0:T(8,128)} %copy.25.sel_ref) | copy-start | bytes 3076
  46.1 19.7 %copy-start.5 = (bf16[2048,128]{1,0:T(8,128)(2,1)S(1)}, bf16[2048,128]{1,0:T(8,128)(2,1)}, u32[]{:S(2)}) copy-start(bf16[2048,128]{1,0:T(8,128)(2,1)} %k0.1) | copy-start | bytes 1572868
  46.1 19.7 %copy-start.6 = (bf16[2048,128]{1,0:T(8,128)(2,1)S(1)}, bf16[2048,128]{1,0:T(8,128)(2,1)}, u32[]{:S(2)}) copy-start(bf16[2048,128]{1,0:T(8,128)(2,1)} %v0.1) | copy-start | bytes 1572868
  53.0 12.8 %collective-permute-start.9 = (bf16[512,128]{1,0:T(8,128)(2,1)S(1)}, bf16[512,128]{1,0:T(8,128)(2,1)S(1)}, u32[]{:S(2)}, u32[]{:S(2)}) collective-permute-start(bf16[512,128]{1,0:T(8,128)(2,1)S(1)} %get-tuple-element.11.n0), channel_id=1, source_target_pairs={{0,32},{32,0},{1,33},{33,1},{2,34},{34,2},{3,35},{35,3},{4,36},{36... | collective-permute-start | bytes 393224 | tf_op jit(solution)/shard_map/ppermute | solution.py:38
  56.4 18.0 %collective-permute-start.15 = (bf16[256,512]{1,0:T(8,128)(2,1)S(1)}, bf16[256,512]{1,0:T(8,128)(2,1)S(1)}, u32[]{:S(2)}, u32[]{:S(2)}) collective-permute-start(bf16[256,512]{1,0:T(8,128)(2,1)S(1)} %get-tuple-element.10.q_ref), channel_id=1, source_target_pairs={{0,128},{64,192},{128,0},{192,64},{1,129},{65,193},{129,1},{193,65... | collective-permute-start | bytes 786440 | tf_op jit(solution)/shard_map/ppermute | solution.py:42
  62.8 27.5 %collective-permute-start.13 = (bf16[256,512]{1,0:T(8,128)(2,1)S(1)}, bf16[256,512]{1,0:T(8,128)(2,1)S(1)}, u32[]{:S(2)}, u32[]{:S(2)}) collective-permute-start(bf16[256,512]{1,0:T(8,128)(2,1)S(1)} %get-tuple-element.10.q_ref), channel_id=1, source_target_pairs={{0,192},{64,0},{128,64},{192,128},{1,193},{65,1},{129,65},{193,129... | collective-permute-start | bytes 786440 | tf_op jit(solution)/shard_map/ppermute | solution.py:42
  63.4 33.8 %collective-permute-start.11 = (bf16[256,512]{1,0:T(8,128)(2,1)S(1)}, bf16[256,512]{1,0:T(8,128)(2,1)S(1)}, u32[]{:S(2)}, u32[]{:S(2)}) collective-permute-start(bf16[256,512]{1,0:T(8,128)(2,1)S(1)} %get-tuple-element.10.q_ref), channel_id=1, source_target_pairs={{0,64},{64,128},{128,192},{192,0},{1,65},{65,129},{129,193},{193,1... | collective-permute-start | bytes 786440 | tf_op jit(solution)/shard_map/ppermute | solution.py:42
  75.7 26.9 %collective-permute-start.16 = (bf16[2,144,512]{2,1,0:T(8,128)(2,1)S(1)}, bf16[2,144,512]{2,1,0:T(8,128)(2,1)S(1)}, u32[]{:S(2)}, u32[]{:S(2)}) collective-permute-start(bf16[2,144,512]{2,1,0:T(8,128)(2,1)S(1)} %attend_other.5), channel_id=1, source_target_pairs={{0,128},{64,192},{128,0},{192,64},{1,129},{65,193},{129,1},{193,65... | collective-permute-start | bytes 884744 | tf_op jit(solution)/shard_map/ppermute | solution.py:42
  97.1 17.0 %collective-permute-start.14 = (bf16[2,144,512]{2,1,0:T(8,128)(2,1)S(1)}, bf16[2,144,512]{2,1,0:T(8,128)(2,1)S(1)}, u32[]{:S(2)}, u32[]{:S(2)}) collective-permute-start(bf16[2,144,512]{2,1,0:T(8,128)(2,1)S(1)} %attend_other.4), channel_id=1, source_target_pairs={{0,64},{64,128},{128,192},{192,0},{1,65},{65,129},{129,193},{193,1... | collective-permute-start | bytes 884744 | tf_op jit(solution)/shard_map/ppermute | solution.py:42
  98.4 15.7 %collective-permute-start.12 = (bf16[2,144,512]{2,1,0:T(8,128)(2,1)S(1)}, bf16[2,144,512]{2,1,0:T(8,128)(2,1)S(1)}, u32[]{:S(2)}, u32[]{:S(2)}) collective-permute-start(bf16[2,144,512]{2,1,0:T(8,128)(2,1)S(1)} %attend_other.3), channel_id=1, source_target_pairs={{0,192},{64,0},{128,64},{192,128},{1,193},{65,1},{129,65},{193,129... | collective-permute-start | bytes 884744 | tf_op jit(solution)/shard_map/ppermute | solution.py:42
